TPU v7x, 32 devices: a whole 2x2x4 slice. The times are simulated.
32 devices in a mesh: var: 8 (over y, x, core), head: 4 (over z).
Axes of the slice: x: 2, y: 2, z: 4, core: 2. Of those that a mesh axis runs over, the one named last changes fastest.
Arguments:
- series: float32 [1024, 8192], P('var', 'head'), may hold values from -48 to 48
- emb_weight: float32 [8192, 512], P('head'), as said below
- emb_bias: float32 [512], replicated, may hold values from -3 to 3
- q_weight: float32 [512, 512], P(None, 'head'), may hold values from -0.75 to 0.75
- k_weight: float32 [512, 512], P(None, 'head'), may hold values from -0.25 to 0.25
- v_weight: float32 [512, 512], P(None, 'head'), may hold values from -0.25 to 0.25
- out_weight: float32 [512, 512], P('head'), may hold values from -0.25 to 0.25
- norm1_gain: float32 [512], replicated, may hold values from 0.1 to 1.9
- norm1_bias: float32 [512], replicated, may hold values from -3 to 3
- ffn_in: float32 [512, 2048], P(None, 'head'), may hold values from -0.25 to 0.25
- ffn_out: float32 [2048, 512], P('head'), may hold values from -0.1875 to 0.1875
- norm2_gain: float32 [512], replicated, may hold values from 0.1 to 1.9
- norm2_bias: float32 [512], replicated, may hold values from -3 to 3
Outputs:
- final: float32 [512, 1024], P('head', 'var')
Inputs may be any that keep to these rules, and one draw needn't show every extreme that they name: `emb_weight`: every entry lies within 12 / sqrt(8192) in magnitude, and some entry reaches that bound.
All inputs are finite; a program needn't handle non-finite values.
Results may differ from a plain program's by a relative error of at most 0.0003.
Values sent between devices are 32-bit elements; how exact they have to be, the bound alone decides.
No kernel may reach another device: no remote copies, remote signals or barrier semaphores. Data moves between devices by JAX's collectives and lax.ppermute only.
A program may use at most 64 MiB of HBM per device.

v0:
```python
import math
import jax
import jax.numpy as jnp
from jax import lax
from jax.sharding import PartitionSpec as P

DH = 64
HIGH = lax.Precision.HIGHEST


def product(first_op, second_op):
    return jnp.dot(first_op, second_op, precision=HIGH, preferred_element_type=jnp.float32)


def project_cols(weight, stream):
    return lax.dot_general(
        weight, stream, (((0,), (1,)), ((), ())), precision=HIGH, preferred_element_type=jnp.float32
    )


def layer_norm(stream, scale_gain, shift_bias):
    centre = jnp.mean(stream, axis=-1, keepdims=True)
    spread = stream - centre
    variance = jnp.mean(spread * spread, axis=-1, keepdims=True)
    return spread * lax.rsqrt(variance + 1e-05) * scale_gain + shift_bias


def fold_keys(state, pieces, queries, local_heads):
    key_piece, value_piece = pieces
    piece_len = key_piece.shape[1]
    block_count = max(1, piece_len // 1024)
    while piece_len % block_count:
        block_count += 1
    block_len = piece_len // block_count
    score_scale = 1.0 / math.sqrt(DH)

    def advance(block_num, carry):
        run_max, run_sum, run_acc = carry
        key_block = lax.dynamic_slice_in_dim(
            key_piece, block_num * block_len, block_len, 1
        ).reshape(local_heads, DH, block_len)
        value_block = lax.dynamic_slice_in_dim(
            value_piece, block_num * block_len, block_len, 1
        ).reshape(local_heads, DH, block_len)
        scores = (
            jnp.einsum(
                "hdk,hdq->hkq",
                key_block,
                queries,
                precision=HIGH,
                preferred_element_type=jnp.float32,
            )
            * score_scale
        )
        new_max = jnp.maximum(run_max, jnp.max(scores, axis=1))
        weights = jnp.exp(scores - new_max[:, None, :])
        rescale = jnp.exp(run_max - new_max)
        new_sum = run_sum * rescale + jnp.sum(weights, axis=1)
        new_acc = run_acc * rescale[:, None, :] + jnp.einsum(
            "hdk,hkq->hdq", value_block, weights, precision=HIGH, preferred_element_type=jnp.float32
        )
        return (new_max, new_sum, new_acc)

    return lax.fori_loop(0, block_count, advance, state)


def on_device(
    series,
    emb_weight,
    emb_bias,
    q_weight,
    k_weight,
    v_weight,
    out_weight,
    norm1_gain,
    norm1_bias,
    ffn_in,
    ffn_out,
    norm2_gain,
    norm2_bias,
):
    head_count = lax.axis_size("head")
    head_pos = lax.axis_index("head")
    model_width = emb_bias.shape[0]
    col_count = model_width // head_count
    col_start = head_pos * col_count
    partial_emb = product(series, emb_weight)
    embedded = lax.psum(partial_emb, "head") + emb_bias
    query_count = embedded.shape[0]
    local_heads = q_weight.shape[1] // DH
    queries = project_cols(q_weight, embedded).reshape(local_heads, DH, query_count)
    key_t = project_cols(k_weight, embedded)
    value_t = project_cols(v_weight, embedded)
    start_state = (
        jnp.full((local_heads, query_count), -1e30, jnp.float32),
        jnp.zeros((local_heads, query_count), jnp.float32),
        jnp.zeros((local_heads, DH, query_count), jnp.float32),
    )
    state = fold_keys(
        start_state,
        (
            lax.all_gather(key_t, "var", axis=1, tiled=True),
            lax.all_gather(value_t, "var", axis=1, tiled=True),
        ),
        queries,
        local_heads,
    )
    run_max, run_sum, run_acc = state
    mixed_t = (run_acc / run_sum[:, None, :]).reshape(local_heads * DH, query_count)
    partial_out = lax.dot_general(
        mixed_t,
        out_weight,
        (((0,), (0,)), ((), ())),
        precision=HIGH,
        preferred_element_type=jnp.float32,
    )
    attention = lax.psum(partial_out, "head")
    normed = layer_norm(embedded + attention, norm1_gain, norm1_bias)
    hidden = jax.nn.gelu(product(normed, ffn_in), approximate=False)
    ffn_t = lax.psum_scatter(
        lax.dot_general(
            ffn_out,
            hidden,
            (((0,), (1,)), ((), ())),
            precision=HIGH,
            preferred_element_type=jnp.float32,
        ),
        "head",
        scatter_dimension=0,
        tiled=True,
    )
    resid_t = lax.dynamic_slice_in_dim(normed, col_start, col_count, 1).T + ffn_t
    col_sums = lax.psum((jnp.sum(resid_t, axis=0), jnp.sum(resid_t * resid_t, axis=0)), "head")
    centre = col_sums[0] / model_width
    variance = col_sums[1] / model_width - centre * centre
    gain_part = lax.dynamic_slice_in_dim(norm2_gain, col_start, col_count)
    bias_part = lax.dynamic_slice_in_dim(norm2_bias, col_start, col_count)
    return (resid_t - centre[None, :]) * lax.rsqrt(variance[None, :] + 1e-05) * gain_part[
        :, None
    ] + bias_part[:, None]


def solution(mesh):
    return jax.shard_map(
        on_device,
        mesh=mesh,
        in_specs=(
            P("var", "head"),
            P("head", None),
            P(),
            P(None, "head"),
            P(None, "head"),
            P(None, "head"),
            P("head", None),
            P(),
            P(),
            P(None, "head"),
            P("head", None),
            P(),
            P(),
        ),
        out_specs=P("head", "var"),
        check_vma=False,
    )
```

profile of v0, /device:TPU:0, one launch (start us, length us, event | category | flops | bytes accessed | tf_op | source)
XLA Modules:
  0.0 158.4 jit_solution(4958936107451321450)
XLA Ops:
  6.6 1.2 copy-done
  7.8 5.3 %fusion.132 = f32[128,512]{1,0:T(8,128)} fusion(f32[128,2048]{1,0:T(8,128)S(1)} %copy-done, f32[2048,512]{1,0:T(8,128)} %param.14), kind=kOutput, calls=%fused_computation.155 | convolution fusion | flops 1610612736 | bytes 5505024 | tf_op jit(solution)/shard_map/dot_general | solution.py:12
  13.2 38.4 %all-reduce.4.cloned.1.call-done = f32[128,512]{1,0:T(8,128)} async-done(((f32[128,512]{1,0:T(8,128)}), f32[128,512]{1,0:T(8,128)}) %all-reduce.4.cloned.1.call-update) | async-done | bytes 262160 | tf_op jit(solution)/shard_map/psum | solution.py:88
  51.6 1.4 convolution_bitcast_fusion.2
  53.0 9.8 %all_gather.6 = f32[128,1024]{0,1:T(8,128)S(1)} all-gather(f32[128,128]{0,1:T(8,128)S(1)} %convolution_bitcast_fusion.2), channel_id=1, replica_groups=mesh['var'=8,'head'=4] {'var'}, dimensions={1}, use_global_device_ids=true | all-gather | bytes 589824 | tf_op jit(solution)/shard_map/all_gather | solution.py:102
  62.8 0.2 copy.17
  63.1 1.5 fusion.62
  64.6 1.8 %fusion.131 = (f32[2,128]{1,0:T(2,128)S(1)}, f32[2,1024,128]{2,1,0:T(8,128)S(1)}) fusion(f32[2,64,1024]{2,1,0:T(8,128)S(1)} %bitcast.29, f32[2,64,128]{2,1,0:T(8,128)S(1)} %bitcast.31), kind=kOutput, calls=%fused_computation.154 | convolution fusion | flops 201850624 | bytes 1639424 | tf_op jit(solution)/shard_map/while/body/eval_jaxpr/hdk,hdq->hkq/dot_general | solution.py:46
  66.6 0.4 convolution_bitcast_fusion.1
  67.0 9.8 %all_gather.7 = f32[128,1024]{0,1:T(8,128)S(1)} all-gather(f32[128,128]{0,1:T(8,128)S(1)} %convolution_bitcast_fusion.1), channel_id=1, replica_groups=mesh['var'=8,'head'=4] {'var'}, dimensions={1}, use_global_device_ids=true | all-gather | bytes 589824 | tf_op jit(solution)/shard_map/all_gather | solution.py:103
  76.9 0.2 copy.18
  77.1 0.9 fusion
  77.9 2.1 %fusion.133 = f32[128,512]{1,0:T(8,128)} fusion(f32[128,128]{1,0:T(8,128)S(1)} %bitcast.30, f32[128,512]{1,0:T(8,128)} %param.19), kind=kOutput, calls=%fused_computation.156 | convolution fusion | flops 100663296 | bytes 589824 | tf_op jit(solution)/shard_map/dot_general | solution.py:110
  80.1 34.6 %all-reduce.6.cloned.1.call-done = f32[128,512]{1,0:T(8,128)} async-done(((f32[128,512]{1,0:T(8,128)}), f32[128,512]{1,0:T(8,128)}) %all-reduce.6.cloned.1.call-update) | async-done | bytes 262160 | tf_op jit(solution)/shard_map/psum | solution.py:117
  114.7 1.1 fusion.130
  115.8 0.2 multiply_reduce_fusion
  116.1 1.9 %fusion.134 = f32[128,512]{1,0:T(8,128)S(1)} fusion(f32[128,512]{1,0:T(8,128)S(1)} %multiply_add_fusion, f32[512,512]{1,0:T(8,128)} %param.22), kind=kOutput, calls=%fused_computation.157 | convolution fusion | flops 402653184 | bytes 1572864 | tf_op jit(solution)/shard_map/dot_general | solution.py:12
  118.1 3.2 %convolution_bitcast_fusion = f32[512,128]{0,1:T(8,128)} fusion(f32[512,512]{1,0:T(8,128)} %param.23, f32[128,512]{1,0:T(8,128)S(1)} %fusion.134), kind=kOutput, calls=%fused_computation.1 | convolution fusion | flops 406847488 | bytes 1572864 | tf_op jit(solution)/shard_map/dot_general | solution.py:121
  121.3 0.8 dynamic_slice.14
  122.1 0.8 dynamic_slice.15
  122.8 18.5 %reduce-scatter.2.cloned.1.call-done = f32[128,128]{0,1:T(8,128)} async-done(((f32[512,128]{0,1:T(8,128)}), f32[128,128]{0,1:T(8,128)}) %reduce-scatter.2.cloned.1.call-update) | async-done | bytes 65552 | tf_op jit(solution)/shard_map/reduce_scatter | solution.py:120
  141.3 1.0 fusion.129
  142.3 8.8 %all-reduce = (f32[128]{0:T(128)S(1)}, f32[128]{0:T(128)S(1)}) all-reduce(f32[128]{0:T(128)S(1)} %get-tuple-element.20, f32[128]{0:T(128)S(1)} %get-tuple-element.19), channel_id=1, replica_groups=mesh['var'=8,'head'=4] {'head'}, use_global_device_ids=true, to_apply=%region_10.0 | all-reduce | flops 256 | bytes 2048 | tf_op jit(solution)/shard_map/psum | solution.py:133
  151.2 0.7 copy.19
  (29 shorter events, 0.6 us)
Async XLA Ops:
  6.5 1.2 copy-start
  6.5 45.1 %copy-start.5 = (f32[512]{0:T(512)S(1)}, f32[512]{0:T(512)}, u32[]{:S(2)}) copy-start(f32[512]{0:T(512)} %param.15) | copy-start | bytes 6148
  6.5 45.1 %copy-start.2 = (f32[512,128]{1,0:T(8,128)S(1)}, f32[512,128]{1,0:T(8,128)}, u32[]{:S(2)}) copy-start(f32[512,128]{1,0:T(8,128)} %param.17) | copy-start | bytes 786436
  6.5 56.5 %copy-start.3 = (f32[512,128]{1,0:T(8,128)S(1)}, f32[512,128]{1,0:T(8,128)}, u32[]{:S(2)}) copy-start(f32[512,128]{1,0:T(8,128)} %param.16) | copy-start | bytes 786436
  6.5 45.1 %all-reduce.4.cloned.1.call-start = ((), (), s32[]{:S(2)}) async-start(), calls=%async_computation.1 | async-start | bytes 524288 | tf_op jit(solution)/shard_map/psum | solution.py:88
  13.1 53.5 %copy-start.4 = (f32[512,128]{1,0:T(8,128)S(1)}, f32[512,128]{1,0:T(8,128)}, u32[]{:S(2)}) copy-start(f32[512,128]{1,0:T(8,128)} %param.18) | copy-start | bytes 786436
  13.1 101.6 %all-reduce.6.cloned.1.call-start = ((), (), s32[]{:S(2)}) async-start(), calls=%async_computation.2 | async-start | bytes 524288 | tf_op jit(solution)/shard_map/psum | solution.py:117
  51.6 15.0 %copy-start.1 = (f32[128,512]{1,0:T(8,128)S(1)}, f32[128,512]{1,0:T(8,128)}, u32[]{:S(2)}) copy-start(f32[128,512]{1,0:T(8,128)} %all-reduce.4.cloned.1.call-done) | copy-start | bytes 786436
  64.6 51.4 %copy-start.6 = (f32[512]{0:T(512)S(1)}, f32[512]{0:T(512)}, u32[]{:S(2)}) copy-start(f32[512]{0:T(512)} %param.21) | copy-start | bytes 6148
  64.6 51.4 %copy-start.7 = (f32[512]{0:T(512)S(1)}, f32[512]{0:T(512)}, u32[]{:S(2)}) copy-start(f32[512]{0:T(512)} %param.20) | copy-start | bytes 6148
  80.0 61.3 %reduce-scatter.2.cloned.1.call-start = ((), (), s32[]{:S(2)}) async-start(), calls=%async_computation.3 | async-start | bytes 327680 | tf_op jit(solution)/shard_map/reduce_scatter | solution.py:120
Sparse Core Ops, SparseCore 0:
  13.2 38.3 all-reduce.3
  80.1 34.5 all-reduce.5
  121.4 19.8 reduce-scatter.1
where the time goes:
time: 159 us; the launch traced here: 158 us
  waiting for transfers between devices  91.6 us (58%)
  blocking collectives  28.4 us (18%)
  matrix products  18.6 us (12%)
  between operations  13.3 us (8%)
  local copies, waits for them, and re-layouts  3.84 us (2%)
  other arithmetic  2.62 us (2%)
    psum x1, waiting for transfers between devices, on_device(): embedded = lax.psum(partial_emb, 'head') + emb_bias  38.4 us
    psum x1, waiting for transfers between devices, on_device(): attention = lax.psum(partial_out, 'head')  34.6 us
    reduce_scatter x1, waiting for transfers between devices, on_device(): lax.psum_scatter(lax.dot_general(ffn_out, hidden, (((0,), (1,)), ((), ())...  18.5 us
    all_gather x1, blocking collectives, on_device(): lax.all_gather(key_t, 'var', axis=1, tiled=True)  9.81 us
    all_gather x1, blocking collectives, on_device(): lax.all_gather(value_t, 'var', axis=1, tiled=True)  9.81 us
    psum x1, blocking collectives, on_device(): lax.psum((jnp.sum(resid_t, axis=0), jnp.sum(resid_t * resid_t, axis=0)),...  8.75 us
    dot_general x2, matrix products, product(): jnp.dot(first_op, second_op, precision=HIGH, preferred_element_type=jnp.f...  7.26 us
    dot_general x3, matrix products, project_cols(): lax.dot_general(weight, stream, (((0,), (1,)), ((), ())), precision=HIGH,...  3.35 us
  transfers between devices with their start and end apart: 3, of which 3 were waited for; matrix products, arithmetic and copies ran while one was open for 1% of the time, Pallas kernels for 0%

commit v1 on v0

--- a/solution.py
+++ b/solution.py
@@ -6,6 +6,18 @@
 
 DH = 64
 HIGH = lax.Precision.HIGHEST
+
+
+def gather_by_bits(array, axis, dim):
+    ways, here, step = (lax.axis_size(axis), lax.axis_index(axis), array.shape[dim])
+    line, have = (array, 1)
+    while have < ways:
+        line = jnp.concatenate(
+            [line, lax.ppermute(line, axis, [(d, (d - have) % ways) for d in range(ways)])],
+            axis=dim,
+        )
+        have = 2 * have
+    return jnp.roll(line, here * step, axis=dim)
 
 
 def product(first_op, second_op):
@@ -98,10 +110,7 @@
     )
     state = fold_keys(
         start_state,
-        (
-            lax.all_gather(key_t, "var", axis=1, tiled=True),
-            lax.all_gather(value_t, "var", axis=1, tiled=True),
-        ),
+        (gather_by_bits(key_t, "var", 1), lax.all_gather(value_t, "var", axis=1, tiled=True)),
         queries,
         local_heads,
     )

time: 159 us -> 164 us (1.031)
  blocking collectives: 28.4 us -> 22.2 us
  local copies, waits for them, and re-layouts: 3.84 us -> 9.56 us
  starting transfers between devices: 0.12 us -> 3.81 us
  waiting for transfers between devices: 91.6 us -> 94.3 us
    all_gather x1 -> x0, blocking collectives: 9.81 us -> none  [on_device(): lax.all_gather(key_t, 'var', axis=1, tiled=True)]
    unnamed x16 -> x26, local copies, waits for them, and re-layouts: 1.21 us -> 5.1 us
    ppermute x0 -> x3, starting transfers between devices: none -> 3.69 us  [gather_by_bits(): lax.ppermute(line, axis, [(d, (d - have) % ways) for d in range(ways)])]
    all_gather x1, blocking collectives: 9.81 us -> 13.4 us  [on_device(): lax.all_gather(value_t, 'var', axis=1, tiled=True)]
    ppermute x0 -> x3, waiting for transfers between devices: none -> 2.63 us  [gather_by_bits(): lax.ppermute(line, axis, [(d, (d - have) % ways) for d in range(ways)])]
  transfers between devices with their start and end apart: 3 -> 6, of which waited for: 3 -> 5; matrix products, arithmetic and copies ran while one was open for 1% -> 4% of each run, Pallas kernels for 0% -> 0%
where the time goes in v1:
time: 164 us
  waiting for transfers between devices  94.3 us (58%)
  blocking collectives  22.2 us (14%)
  matrix products  17.9 us (11%)
  between operations  13.3 us (8%)
  local copies, waits for them, and re-layouts  9.56 us (6%)
  starting transfers between devices  3.81 us (2%)
  other arithmetic  2.64 us (2%)
    psum x1, waiting for transfers between devices, on_device(): embedded = lax.psum(partial_emb, 'head') + emb_bias  38.4 us
    psum x1, waiting for transfers between devices, on_device(): attention = lax.psum(partial_out, 'head')  34.7 us
    reduce_scatter x1, waiting for transfers between devices, on_device(): lax.psum_scatter(lax.dot_general(ffn_out, hidden, (((0,), (1,)), ((), ())...  18.5 us
    all_gather x1, blocking collectives, on_device(): lax.all_gather(value_t, 'var', axis=1, tiled=True)  13.4 us
    psum x1, blocking collectives, on_device(): lax.psum((jnp.sum(resid_t, axis=0), jnp.sum(resid_t * resid_t, axis=0)),...  8.84 us
    dot_general x2, matrix products, product(): jnp.dot(first_op, second_op, precision=HIGH, preferred_element_type=jnp.f...  6.03 us
    unnamed x26, local copies, waits for them, and re-layouts  5.1 us
    dot_general x3, matrix products, project_cols(): lax.dot_general(weight, stream, (((0,), (1,)), ((), ())), precision=HIGH,...  4.85 us
  transfers between devices with their start and end apart: 6, of which 5 were waited for; matrix products, arithmetic and copies ran while one was open for 4% of the time, Pallas kernels for 0%

profile of v1, /device:TPU:0, one launch (start us, length us, event | category | flops | bytes accessed | tf_op | source)
XLA Modules:
  0.0 163.7 jit_solution(964568007458419702)
XLA Ops:
  6.6 1.2 copy-done
  7.8 5.3 %fusion.132 = f32[128,512]{1,0:T(8,128)} fusion(f32[128,2048]{1,0:T(8,128)S(1)} %copy-done, f32[2048,512]{1,0:T(8,128)} %param.14), kind=kOutput, calls=%fused_computation.166 | convolution fusion | flops 1610612736 | bytes 5505024 | tf_op jit(solution)/shard_map/dot_general | solution.py:24
  13.2 38.4 %all-reduce.4.cloned.1.call-done = f32[128,512]{1,0:T(8,128)} async-done(((f32[128,512]{1,0:T(8,128)}), f32[128,512]{1,0:T(8,128)}) %all-reduce.4.cloned.1.call-update) | async-done | bytes 262160 | tf_op jit(solution)/shard_map/psum | solution.py:100
  51.6 2.0 %constant_dynamic-update-slice_fusion.7 = (f32[128,2048]{0,1:T(8,128)}, f32[128,128]{0,1:T(8,128)S(1)}) fusion(f32[512,128]{1,0:T(8,128)S(1)} %copy-done.3, f32[128,512]{1,0:T(8,128)} %all-reduce.4.cloned.1.call-done, f32[512]{0:T(512)S(1)} %copy-done.7), kind=kOutput, calls=%fused_computation.124 | convolution fusion | flops 100728832 | bytes 657408 | tf_op jit(solution)/shard_map/dot_general | solution.py:28
  53.6 1.5 fusion.62
  55.5 2.4 %collective-permute-start.1 = (f32[128,256]{0,1:T(8,128)S(1)}, f32[128,256]{0,1:T(8,128)S(1)}, u32[]{:S(2)}, u32[]{:S(2)}) collective-permute-start(f32[128,256]{0,1:T(8,128)S(1)} %pad_maximum_fusion.1), channel_id=1, source_target_pairs={{0,24},{4,28},{8,0},{12,4},{16,8},{20,12},{24,16},{28,20},{1,25},{... | collective-permute-start | bytes 393224 | tf_op jit(solution)/shard_map/ppermute | solution.py:16
  57.9 1.3 convolution_bitcast_fusion.1
  59.3 2.3 %collective-permute-done.1 = f32[128,256]{0,1:T(8,128)S(1)} collective-permute-done((f32[128,256]{0,1:T(8,128)S(1)}, f32[128,256]{0,1:T(8,128)S(1)}, u32[]{:S(2)}, u32[]{:S(2)}) %collective-permute-start.1) | collective-permute-done | bytes 131104 | tf_op jit(solution)/shard_map/ppermute | solution.py:16
  61.6 1.3 collective-permute-start.2
  62.8 13.4 %all_gather.3 = f32[128,1024]{0,1:T(8,128)S(1)} all-gather(f32[128,128]{0,1:T(8,128)S(1)} %convolution_bitcast_fusion.1), channel_id=1, replica_groups=mesh['var'=8,'head'=4] {'var'}, dimensions={1}, use_global_device_ids=true | all-gather | bytes 589824 | tf_op jit(solution)/shard_map/all_gather | solution.py:113
  80.3 0.7 constant_dynamic-update-slice_fusion
  81.0 1.1 constant_dynamic-slice_fusion
  82.4 1.8 %fusion.131 = (f32[2,128]{1,0:T(2,128)S(1)}, f32[2,1024,128]{2,1,0:T(8,128)S(1)}) fusion(f32[2,64,1024]{2,1,0:T(8,128)S(1)} %bitcast.29, f32[2,64,128]{2,1,0:T(8,128)S(1)} %bitcast.30), kind=kOutput, calls=%fused_computation.165 | convolution fusion | flops 201850624 | bytes 1639424 | tf_op jit(solution)/shard_map/while/body/eval_jaxpr/hdk,hdq->hkq/dot_general | solution.py:58
  84.4 0.9 fusion
  85.2 1.1 fusion.133
  86.4 34.7 %all-reduce.6.cloned.1.call-done = f32[128,512]{1,0:T(8,128)} async-done(((f32[128,512]{1,0:T(8,128)}), f32[128,512]{1,0:T(8,128)}) %all-reduce.6.cloned.1.call-update) | async-done | bytes 262160 | tf_op jit(solution)/shard_map/psum | solution.py:126
  121.1 1.1 fusion.130
  123.3 3.2 %convolution_bitcast_fusion = f32[512,128]{0,1:T(8,128)} fusion(f32[512,512]{1,0:T(8,128)} %param.23, f32[128,512]{1,0:T(8,128)S(1)} %fusion.134), kind=kOutput, calls=%fused_computation.1 | convolution fusion | flops 406847488 | bytes 1572864 | tf_op jit(solution)/shard_map/dot_general | solution.py:130
  126.5 0.8 dynamic_slice.19
  127.3 0.8 dynamic_slice.20
  128.0 18.5 %reduce-scatter.2.cloned.1.call-done = f32[128,128]{0,1:T(8,128)} async-done(((f32[512,128]{0,1:T(8,128)}), f32[128,128]{0,1:T(8,128)}) %reduce-scatter.2.cloned.1.call-update) | async-done | bytes 65552 | tf_op jit(solution)/shard_map/reduce_scatter | solution.py:129
  146.5 1.0 fusion.129
  147.5 8.8 %all-reduce = (f32[128]{0:T(128)S(1)}, f32[128]{0:T(128)S(1)}) all-reduce(f32[128]{0:T(128)S(1)} %get-tuple-element.20, f32[128]{0:T(128)S(1)} %get-tuple-element.19), channel_id=1, replica_groups=mesh['var'=8,'head'=4] {'head'}, use_global_device_ids=true, to_apply=%region_10.11 | all-reduce | flops 256 | bytes 2048 | tf_op jit(solution)/shard_map/psum | solution.py:142
  156.4 0.7 copy.18
  (48 shorter events, 6.2 us)
Async XLA Ops:
  6.5 1.2 copy-start
  6.5 45.1 %copy-start.7 = (f32[512]{0:T(512)S(1)}, f32[512]{0:T(512)}, u32[]{:S(2)}) copy-start(f32[512]{0:T(512)} %param.15) | copy-start | bytes 6148
  6.5 45.1 %copy-start.3 = (f32[512,128]{1,0:T(8,128)S(1)}, f32[512,128]{1,0:T(8,128)}, u32[]{:S(2)}) copy-start(f32[512,128]{1,0:T(8,128)} %param.17) | copy-start | bytes 786436
  6.5 47.0 %copy-start.4 = (f32[512,128]{1,0:T(8,128)S(1)}, f32[512,128]{1,0:T(8,128)}, u32[]{:S(2)}) copy-start(f32[512,128]{1,0:T(8,128)} %param.16) | copy-start | bytes 786436
  6.5 51.4 %copy-start.5 = (f32[512,128]{1,0:T(8,128)S(1)}, f32[512,128]{1,0:T(8,128)}, u32[]{:S(2)}) copy-start(f32[512,128]{1,0:T(8,128)} %param.18) | copy-start | bytes 786436
  6.5 45.0 %all-reduce.4.cloned.1.call-start = ((), (), s32[]{:S(2)}) async-start(), calls=%async_computation.1 | async-start | bytes 524288 | tf_op jit(solution)/shard_map/psum | solution.py:100
  13.1 108.0 %all-reduce.6.cloned.1.call-start = ((), (), s32[]{:S(2)}) async-start(), calls=%async_computation.2 | async-start | bytes 524288 | tf_op jit(solution)/shard_map/psum | solution.py:126
  53.6 1.9 %collective-permute-start = (f32[128,128]{0,1:T(8,128)S(1)}, f32[128,128]{0,1:T(8,128)S(1)}, u32[]{:S(2)}, u32[]{:S(2)}) collective-permute-start(f32[128,128]{0,1:T(8,128)S(1)} %get-tuple-element.41), channel_id=1, source_target_pairs={{0,28},{4,0},{8,4},{12,8},{16,12},{20,16},{24,20},{28,24},{1,29},{... | collective-permute-start | bytes 196616 | tf_op jit(solution)/shard_map/ppermute | solution.py:16
  55.5 6.1 %collective-permute-start.1 = (f32[128,256]{0,1:T(8,128)S(1)}, f32[128,256]{0,1:T(8,128)S(1)}, u32[]{:S(2)}, u32[]{:S(2)}) collective-permute-start(f32[128,256]{0,1:T(8,128)S(1)} %pad_maximum_fusion.1), channel_id=1, source_target_pairs={{0,24},{4,28},{8,0},{12,4},{16,8},{20,12},{24,16},{28,20},{1,25},{... | collective-permute-start | bytes 393224 | tf_op jit(solution)/shard_map/ppermute | solution.py:16
  61.6 16.1 %collective-permute-start.2 = (f32[128,512]{0,1:T(8,128)S(1)}, f32[128,512]{0,1:T(8,128)S(1)}, u32[]{:S(2)}, u32[]{:S(2)}) collective-permute-start(f32[128,512]{0,1:T(8,128)S(1)} %pad_maximum_fusion), channel_id=1, source_target_pairs={{0,16},{4,20},{8,24},{12,28},{16,0},{20,4},{24,8},{28,12},{1,17},{... | collective-permute-start | bytes 786440 | tf_op jit(solution)/shard_map/ppermute | solution.py:16
  76.4 8.8 %copy-start.6 = (f32[128,512]{1,0:T(8,128)S(1)}, f32[128,512]{1,0:T(8,128)}, u32[]{:S(2)}) copy-start(f32[128,512]{1,0:T(8,128)} %param.19) | copy-start | bytes 786436
  78.4 42.7 %copy-start.1 = (f32[128,512]{1,0:T(8,128)S(1)}, f32[128,512]{1,0:T(8,128)}, u32[]{:S(2)}) copy-start(f32[128,512]{1,0:T(8,128)} %all-reduce.4.cloned.1.call-done) | copy-start | bytes 786436
  81.0 41.3 %copy-start.8 = (f32[512]{0:T(512)S(1)}, f32[512]{0:T(512)}, u32[]{:S(2)}) copy-start(f32[512]{0:T(512)} %param.21) | copy-start | bytes 6148
  81.0 41.3 %copy-start.9 = (f32[512]{0:T(512)S(1)}, f32[512]{0:T(512)}, u32[]{:S(2)}) copy-start(f32[512]{0:T(512)} %param.20) | copy-start | bytes 6148
  84.2 38.3 %copy-start.2 = (f32[512,512]{1,0:T(8,128)S(1)}, f32[512,512]{1,0:T(8,128)}, u32[]{:S(2)}) copy-start(f32[512,512]{1,0:T(8,128)} %param.22) | copy-start | bytes 3145732
  86.4 60.1 %reduce-scatter.2.cloned.1.call-start = ((), (), s32[]{:S(2)}) async-start(), calls=%async_computation.3 | async-start | bytes 327680 | tf_op jit(solution)/shard_map/reduce_scatter | solution.py:129
Sparse Core Ops, SparseCore 0:
  13.2 38.3 all-reduce.3
  86.5 34.5 all-reduce.5
  126.6 19.8 reduce-scatter.1
